TPU v7x, 32 devices: a whole 2x2x4 slice. The times are simulated.
32 devices in a mesh: group: 2 (over x), module: 16 (over z, y, core).
Axes of the slice: x: 2, y: 2, z: 4, core: 2. Of those that a mesh axis runs over, the one named last changes fastest.
Arguments:
- query_grads: float32 [16, 32, 128, 128], P(None, None, 'module'), may hold values from -0.1875 to 0.1875
- train_grads: float32 [32, 128, 128, 128], P('module', 'group'), parts along dimension 1, may hold values from -0.1875 to 0.1875
- out_basis: float32 [32, 128, 128], P('module'), may hold values from -0.5 to 0.5
- in_basis: float32 [32, 128, 128], P('module'), may hold values from -0.5 to 0.5
- corrections: float32 [32, 128, 128], P('module'), may hold values from 0.01 to 10
- ranks: int32 [16], replicated, may hold values from 32 to 128
- slot_modules: int32 [32], replicated, may hold values from -1 to 15, as said below
Outputs:
- scores: float32 [32, 128], P(None, 'group'), parts along dimension 1
There are 2 independent parts, one for each index of `group`. A program takes and returns all parts, laid end to end along the dimension named above; an argument that names none is the same for every part. Nothing has to cross between parts.
Inputs may be any that keep to these rules, and one draw needn't show every extreme that they name: `slot_modules`: each module number 0 to 15 stands in exactly one entry; all other entries are -1. Owner i holds the 2 entries from i * 2 on, so an owner holds 0 to 2 modules, and some owner holds 2.
All inputs are finite; a program needn't handle non-finite values.
Results may differ from a plain program's by a relative error of at most 0.0003.
Values sent between devices are 32-bit elements; how exact they have to be, the bound alone decides.
No kernel may reach another device: no remote copies, remote signals or barrier semaphores. Data moves between devices by JAX's collectives and lax.ppermute only.
A program may use at most 128 MiB of HBM per device.

v0:
```python
import jax
import jax.numpy as jnp
from jax import lax
from jax.sharding import PartitionSpec as P


def rotate(field, output_eigenbasis, inner_basis):
    inner = jnp.einsum("noi,ib->nob", field, inner_basis, precision=lax.Precision.HIGHEST)
    return jnp.einsum("oa,nob->nab", output_eigenbasis, inner, precision=lax.Precision.HIGHEST)


def blank_rotation(field, output_eigenbasis, inner_basis):
    return jnp.zeros(field.shape, jnp.float32)


def slot_weight(spectrum, keep_rank):
    damping = 0.1 * jnp.mean(spectrum)
    positions = lax.iota(jnp.int32, spectrum.shape[0])
    kept_mask = (positions[:, None] < keep_rank) & (positions[None, :] < keep_rank)
    return jnp.where(kept_mask, 1.0 / (spectrum + damping), jnp.zeros_like(spectrum))


def score_rotated(query_block, rotated_train, output_eigenbasis, inner_basis, spectrum, keep_rank):
    scaled = rotate(query_block, output_eigenbasis, inner_basis) * slot_weight(spectrum, keep_rank)
    return jnp.einsum("qab,eab->qe", scaled, rotated_train, precision=lax.Precision.HIGHEST)


def blank_scores(query_block, second_block, output_eigenbasis, inner_basis, spectrum, keep_rank):
    return jnp.zeros((query_block.shape[0], second_block.shape[0]), jnp.float32)


def body(query_grads, train_grads, out_basis, in_basis, corrections, ranks, slot_modules):
    slot_count = out_basis.shape[0]
    peer_count = lax.axis_size("module")
    own_index = lax.axis_index("module")
    owned_modules = lax.dynamic_slice_in_dim(slot_modules, own_index * slot_count, slot_count)
    query_count = query_grads.shape[1]
    example_count = train_grads.shape[1]
    rotated = []
    for number in range(slot_count):
        rotated.append(
            lax.cond(
                owned_modules[number] >= 0,
                rotate,
                blank_rotation,
                train_grads[number],
                out_basis[number],
                in_basis[number],
            )
        )
    safe_index = jnp.maximum(slot_modules, 0)
    populated_slots = slot_modules >= 0
    outgoing = jnp.where(populated_slots[:, None, None, None], query_grads[safe_index], 0.0)
    outgoing = outgoing.reshape((peer_count, slot_count) + outgoing.shape[1:])
    received = lax.all_to_all(outgoing, "module", split_axis=0, concat_axis=3, tiled=True)[0]
    running = jnp.zeros((query_count, example_count), jnp.float32)
    for number in range(slot_count):
        module = owned_modules[number]
        keep_rank = ranks[jnp.maximum(module, 0)]
        term = lax.cond(
            module >= 0,
            score_rotated,
            blank_scores,
            received[number],
            rotated[number],
            out_basis[number],
            in_basis[number],
            corrections[number],
            keep_rank,
        )
        running = running + term
    return lax.psum(running, "module")


def solution(mesh):
    return jax.shard_map(
        body,
        mesh=mesh,
        in_specs=(
            P(None, None, "module", None),
            P("module", "group", None, None),
            P("module", None, None),
            P("module", None, None),
            P("module", None, None),
            P(),
            P(),
        ),
        out_specs=P(None, "group"),
        check_vma=False,
    )
```

profile of v0, /device:TPU:0, one launch (start us, length us, event | category | flops | bytes accessed | tf_op | source)
XLA Modules:
  0.0 223.0 jit_solution(18283808478415897497)
XLA Ops:
  0.0 0.0 copy-start
  0.0 0.8 broadcast_maximum_fusion
  0.8 0.7 broadcast_compare_fusion
  1.5 0.1 broadcast_in_dim.24
  1.6 0.0 copy-done
  1.6 2.8 %gather_fusion = f32[32,32,8,128]{3,2,1,0:T(8,128)} fusion(f32[16,32,8,128]{3,2,1,0:T(8,128)S(1)} %copy-done, s32[1024]{0:T(1024)S(1)} %pad_clamp_fusion), kind=kCustom, calls=%fused_computation | custom fusion | bytes 8388736 | tf_op jit(solution)/shard_map/gather | solution.py:53
  4.4 4.8 %broadcast_select_fusion = f32[16,2,32,8,128]{4,3,2,1,0:T(8,128)} fusion(f32[16,2,32,8,128]{4,3,2,1,0:T(8,128)} %bitcast.80, pred[16,2]{1,0:T(8,128)(4,1)S(1)} %broadcast_in_dim.24), kind=kLoop, calls=%fused_computation.37 | loop fusion | flops 1048576 | bytes 8388640 | tf_op jit(solution)/shard_map/jit(_where)/select_n | solution.py:53
  9.1 0.0 copy-start.4
  9.1 0.0 copy-start.2
  9.1 0.0 copy-start.3
  9.1 7.6 %all-to-all-start = ((f32[16,2,32,8,128]{4,3,2,1,0:T(8,128)}), f32[16,2,32,8,128]{4,3,2,1,0:T(8,128)}, u32[]{:S(2)}, u32[]{:S(2)}) async-start(f32[16,2,32,8,128]{4,3,2,1,0:T(8,128)} %broadcast_select_fusion), calls=%async_computation | async-start | bytes 8388608 | tf_op jit(solution)/shard_map/all_to_all | solution.py:55
  16.7 0.0 copy-done.4
  16.7 0.1 dynamic_slice.11
  16.8 0.6 fusion.24
  18.7 0.0 copy-done.2
  18.8 0.0 copy-done.3
  18.8 2.5 %conditional.6 = (f32[64,128,128]{1,2,0:T(8,128)}) conditional(s32[]{:T(128)} %convert_element_type.9, () %tuple.34, (f32[2,64,128,128]{3,2,1,0:T(8,128)}, f32[128,128]{1,0:T(8,128)S(1)}, f32[128,128]{1,0:T(8,128)S(1)}) %tuple.35), branch_computations={%region_5.6_spmd, %region_6.0_spmd} | conditional | flops 3221225472 | bytes 16908296 | solution.py:42
  18.8 2.4 %broadcast.55 = f32[64,128,128]{1,2,0:T(8,128)} broadcast(f32[]{:T(128)} %constant.18.clone), dimensions={} | broadcast | bytes 4194308 | tf_op jit(solution)/shard_map/broadcast.4
  21.2 0.0 copy-start.1
  21.2 0.0 copy-start.5
  21.3 2.5 %conditional.4 = (f32[64,128,128]{1,2,0:T(8,128)}) conditional(s32[]{:T(128)} %convert_element_type.8, () %tuple.30, (f32[2,64,128,128]{3,2,1,0:T(8,128)}, f32[128,128]{1,0:T(8,128)S(1)}, f32[128,128]{1,0:T(8,128)S(1)}) %tuple.31), branch_computations={%region_0.0_spmd, %region_1.0_spmd} | conditional | flops 3221225472 | bytes 16908296 | solution.py:42
  21.3 2.5 %broadcast.51 = f32[64,128,128]{1,2,0:T(8,128)} broadcast(f32[]{:T(128)} %constant.8.clone), dimensions={} | broadcast | bytes 4194308 | tf_op jit(solution)/shard_map/broadcast.2
  23.7 70.5 %all-to-all-done = f32[16,2,32,8,128]{4,3,2,1,0:T(8,128)} async-done(((f32[16,2,32,8,128]{4,3,2,1,0:T(8,128)}), f32[16,2,32,8,128]{4,3,2,1,0:T(8,128)}, u32[]{:S(2)}, u32[]{:S(2)}) %all-to-all-start) | async-done | bytes 4194336 | tf_op jit(solution)/shard_map/all_to_all | solution.py:55
  94.3 0.0 copy-done.1
  94.3 0.0 copy-done.5
  94.3 0.2 conditional.7
  94.5 0.2 conditional.5
  94.7 128.2 %psum.7 = f32[32,64]{1,0:T(8,128)} all-reduce(f32[32,64]{1,0:T(8,128)S(1)} %add.27), channel_id=1, replica_groups=mesh['group'=2,'module'=16] {'module'}, use_global_device_ids=true, to_apply=%region_10.11 | all-reduce | flops 2048 | bytes 16384 | tf_op jit(solution)/shard_map/psum | solution.py:72
  (5 shorter events, 0.0 us)
Async XLA Ops:
  0.0 1.6 copy-start
  9.1 7.6 %copy-start.4 = (s32[32]{0:T(128)S(1)}, s32[32]{0:T(128)}, u32[]{:S(2)}) copy-start(s32[32]{0:T(128)} %param.21) | copy-start | bytes 388
  9.1 9.6 %copy-start.2 = (f32[2,128,128]{2,1,0:T(8,128)S(1)}, f32[2,128,128]{2,1,0:T(8,128)}, u32[]{:S(2)}) copy-start(f32[2,128,128]{2,1,0:T(8,128)} %param.17) | copy-start | bytes 393220
  9.1 9.6 %copy-start.3 = (f32[2,128,128]{2,1,0:T(8,128)S(1)}, f32[2,128,128]{2,1,0:T(8,128)}, u32[]{:S(2)}) copy-start(f32[2,128,128]{2,1,0:T(8,128)} %param.18) | copy-start | bytes 393220
  9.1 85.1 %all-to-all-start = ((f32[16,2,32,8,128]{4,3,2,1,0:T(8,128)}), f32[16,2,32,8,128]{4,3,2,1,0:T(8,128)}, u32[]{:S(2)}, u32[]{:S(2)}) async-start(f32[16,2,32,8,128]{4,3,2,1,0:T(8,128)} %broadcast_select_fusion), calls=%async_computation | async-start | bytes 8388608 | tf_op jit(solution)/shard_map/all_to_all | solution.py:55
  21.2 73.0 %copy-start.1 = (f32[2,128,128]{2,1,0:T(8,128)S(1)}, f32[2,128,128]{2,1,0:T(8,128)}, u32[]{:S(2)}) copy-start(f32[2,128,128]{2,1,0:T(8,128)} %param.19) | copy-start | bytes 393220
  21.2 73.0 %copy-start.5 = (s32[16]{0:T(128)S(1)}, s32[16]{0:T(128)}, u32[]{:S(2)}) copy-start(s32[16]{0:T(128)} %param.20) | copy-start | bytes 196
where the time goes:
time: 224 us; the launch traced here: 223 us
  blocking collectives  128 us (57%)
  waiting for transfers between devices  70.5 us (31%)
  local copies, waits for them, and re-layouts  8.53 us (4%)
  starting transfers between devices  7.6 us (3%)
  other arithmetic  6.23 us (3%)
    psum x1, blocking collectives, body(): return lax.psum(running, 'module')  128 us
    all_to_all x1, waiting for transfers between devices, body(): lax.all_to_all(outgoing, 'module', split_axis=0, concat_axis=3, tiled=True)  70.5 us
    all_to_all x1, starting transfers between devices, body(): lax.all_to_all(outgoing, 'module', split_axis=0, concat_axis=3, tiled=True)  7.6 us
    another operation x4, local copies, waits for them, and re-layouts  4.93 us
    select_n x1, other arithmetic, body(): jnp.where(populated_slots[:, None, None, None], query_grads[safe_index],...  4.75 us
  transfers between devices with their start and end apart: 1, of which 1 were waited for; matrix products, arithmetic and copies ran while one was open for 3% of the time, Pallas kernels for 0%

commit v1 on v0

--- a/solution.py
+++ b/solution.py
@@ -52,7 +52,12 @@
     populated_slots = slot_modules >= 0
     outgoing = jnp.where(populated_slots[:, None, None, None], query_grads[safe_index], 0.0)
     outgoing = outgoing.reshape((peer_count, slot_count) + outgoing.shape[1:])
-    received = lax.all_to_all(outgoing, "module", split_axis=0, concat_axis=3, tiled=True)[0]
+    received = jnp.concatenate(
+        lax.all_to_all(
+            jnp.stack(jnp.split(outgoing, lax.axis_size("module"), axis=0)), "module", 0, 0
+        ),
+        axis=3,
+    )[0]
     running = jnp.zeros((query_count, example_count), jnp.float32)
     for number in range(slot_count):
         module = owned_modules[number]

time: 224 us -> 233 us (1.040)
  local copies, waits for them, and re-layouts: 8.53 us -> 20.1 us
    unnamed x12 -> x27, local copies, waits for them, and re-layouts: 0.06 us -> 11 us
    another operation x4 -> x5, local copies, waits for them, and re-layouts: 4.93 us -> 5.69 us
  transfers between devices with their start and end apart: 1 -> 1, of which waited for: 1 -> 1; matrix products, arithmetic and copies ran while one was open for 3% -> 2% of each run, Pallas kernels for 0% -> 0%
where the time goes in v1:
time: 233 us; the launch traced here: 232 us
  blocking collectives  128 us (55%)
  waiting for transfers between devices  70.5 us (30%)
  local copies, waits for them, and re-layouts  20.1 us (9%)
  starting transfers between devices  7.6 us (3%)
  other arithmetic  4.13 us (2%)
    psum x1, blocking collectives, body(): return lax.psum(running, 'module')  128 us
    all_to_all x1, waiting for transfers between devices, body(): lax.all_to_all(jnp.stack(jnp.split(outgoing, lax.axis_size('module'), axi...  70.5 us
    unnamed x27, local copies, waits for them, and re-layouts  11 us
    all_to_all x1, starting transfers between devices, body(): lax.all_to_all(jnp.stack(jnp.split(outgoing, lax.axis_size('module'), axi...  7.6 us
    another operation x4, local copies, waits for them, and re-layouts  4.93 us
  transfers between devices with their start and end apart: 1, of which 1 were waited for; matrix products, arithmetic and copies ran while one was open for 2% of the time, Pallas kernels for 0%

profile of v1, /device:TPU:0, one launch (start us, length us, event | category | flops | bytes accessed | tf_op | source)
XLA Modules:
  0.0 232.5 jit_solution(12734194429731628170)
XLA Ops:
  0.0 0.8 broadcast_maximum_fusion
  0.8 0.7 broadcast_compare_fusion
  1.5 0.1 copy-done
  1.6 2.8 %gather_fusion = f32[32,32,8,128]{3,2,1,0:T(8,128)} fusion(f32[16,32,8,128]{3,2,1,0:T(8,128)S(1)} %copy-done, s32[1024]{0:T(1024)S(1)} %pad_clamp_fusion), kind=kCustom, calls=%fused_computation | custom fusion | bytes 8388736 | tf_op jit(solution)/shard_map/gather | solution.py:53
  4.4 2.7 %broadcast_select_fusion = f32[32,32,8,128]{3,2,1,0:T(8,128)S(1)} fusion(f32[32,32,8,128]{3,2,1,0:T(8,128)} %gather_fusion, pred[32]{0:T(512)(128)(4,1)S(1)} %broadcast_compare_fusion), kind=kLoop, calls=%fused_computation.37 | loop fusion | flops 1048576 | bytes 8388640 | tf_op jit(solution)/shard_map/jit(_where)/select_n | solution.py:53
  7.0 0.7 fusion.39
  7.7 0.7 fusion.38
  8.5 0.7 fusion.37
  9.2 0.7 fusion.36
  9.9 0.7 fusion.35
  10.7 0.7 fusion.34
  11.4 0.7 fusion.33
  12.1 0.7 fusion.32
  12.8 0.7 fusion.31
  13.5 0.7 fusion.30
  14.3 0.7 fusion.29
  15.0 0.7 fusion.28
  15.7 0.7 fusion.27
  16.4 0.7 fusion.26
  17.1 0.7 fusion.25
  17.8 0.8 fusion.24
  18.6 7.6 %all-to-all-start = ((f32[16,1,2,32,8,128]{5,4,3,2,1,0:T(8,128)}), f32[16,1,2,32,8,128]{5,4,3,2,1,0:T(8,128)}, u32[]{:S(2)}, u32[]{:S(2)}) async-start(f32[16,1,2,32,8,128]{5,4,3,2,1,0:T(8,128)} %fusion.24), calls=%async_computation | async-start | bytes 8388608 | tf_op jit(solution)/shard_map/all_to_all | solution.py:56
  26.2 0.1 dynamic_slice.11
  26.3 0.6 fusion.40
  28.3 2.5 %conditional.6 = (f32[64,128,128]{1,2,0:T(8,128)}) conditional(s32[]{:T(128)} %convert_element_type.9, () %tuple.34, (f32[2,64,128,128]{3,2,1,0:T(8,128)}, f32[128,128]{1,0:T(8,128)S(1)}, f32[128,128]{1,0:T(8,128)S(1)}) %tuple.35), branch_computations={%region_5.6_spmd, %region_6.0_spmd} | conditional | flops 3221225472 | bytes 16908296 | solution.py:42
  28.3 2.4 %broadcast.54 = f32[64,128,128]{1,2,0:T(8,128)} broadcast(f32[]{:T(128)} %constant.18.clone), dimensions={} | broadcast | bytes 4194308 | tf_op jit(solution)/shard_map/broadcast.4
  30.7 2.5 %conditional.4 = (f32[64,128,128]{1,2,0:T(8,128)}) conditional(s32[]{:T(128)} %convert_element_type.8, () %tuple.30, (f32[2,64,128,128]{3,2,1,0:T(8,128)}, f32[128,128]{1,0:T(8,128)S(1)}, f32[128,128]{1,0:T(8,128)S(1)}) %tuple.31), branch_computations={%region_0.0_spmd, %region_1.0_spmd} | conditional | flops 3221225472 | bytes 16908296 | solution.py:42
  30.7 2.5 %broadcast.50 = f32[64,128,128]{1,2,0:T(8,128)} broadcast(f32[]{:T(128)} %constant.8.clone), dimensions={} | broadcast | bytes 4194308 | tf_op jit(solution)/shard_map/broadcast.2
  33.2 70.5 %all-to-all-done = f32[16,1,2,32,8,128]{5,4,3,2,1,0:T(8,128)} async-done(((f32[16,1,2,32,8,128]{5,4,3,2,1,0:T(8,128)}), f32[16,1,2,32,8,128]{5,4,3,2,1,0:T(8,128)}, u32[]{:S(2)}, u32[]{:S(2)}) %all-to-all-start) | async-done | bytes 4194336 | tf_op jit(solution)/shard_map/all_to_all | solution.py:56
  103.8 0.2 conditional.7
  104.0 0.2 conditional.5
  104.2 128.3 %psum.7 = f32[32,64]{1,0:T(8,128)} all-reduce(f32[32,64]{1,0:T(8,128)S(1)} %add.27), channel_id=1, replica_groups=mesh['group'=2,'module'=16] {'module'}, use_global_device_ids=true, to_apply=%region_10.11 | all-reduce | flops 2048 | bytes 16384 | tf_op jit(solution)/shard_map/psum | solution.py:77
  (16 shorter events, 0.1 us)
Async XLA Ops:
  0.0 1.6 copy-start
  18.6 7.6 %copy-start.4 = (s32[32]{0:T(128)S(1)}, s32[32]{0:T(128)}, u32[]{:S(2)}) copy-start(s32[32]{0:T(128)} %param.21) | copy-start | bytes 388
  18.6 9.6 %copy-start.2 = (f32[2,128,128]{2,1,0:T(8,128)S(1)}, f32[2,128,128]{2,1,0:T(8,128)}, u32[]{:S(2)}) copy-start(f32[2,128,128]{2,1,0:T(8,128)} %param.17) | copy-start | bytes 393220
  18.6 9.6 %copy-start.3 = (f32[2,128,128]{2,1,0:T(8,128)S(1)}, f32[2,128,128]{2,1,0:T(8,128)}, u32[]{:S(2)}) copy-start(f32[2,128,128]{2,1,0:T(8,128)} %param.18) | copy-start | bytes 393220
  18.6 85.1 %all-to-all-start = ((f32[16,1,2,32,8,128]{5,4,3,2,1,0:T(8,128)}), f32[16,1,2,32,8,128]{5,4,3,2,1,0:T(8,128)}, u32[]{:S(2)}, u32[]{:S(2)}) async-start(f32[16,1,2,32,8,128]{5,4,3,2,1,0:T(8,128)} %fusion.24), calls=%async_computation | async-start | bytes 8388608 | tf_op jit(solution)/shard_map/all_to_all | solution.py:56
  30.7 73.0 %copy-start.1 = (f32[2,128,128]{2,1,0:T(8,128)S(1)}, f32[2,128,128]{2,1,0:T(8,128)}, u32[]{:S(2)}) copy-start(f32[2,128,128]{2,1,0:T(8,128)} %param.19) | copy-start | bytes 393220
  30.7 73.0 %copy-start.5 = (s32[16]{0:T(128)S(1)}, s32[16]{0:T(128)}, u32[]{:S(2)}) copy-start(s32[16]{0:T(128)} %param.20) | copy-start | bytes 196

commit v2 on v0

--- a/solution.py
+++ b/solution.py
@@ -69,7 +69,7 @@
             keep_rank,
         )
         running = running + term
-    return lax.psum(running, "module")
+    return jnp.sum(lax.all_gather(running, "module"), axis=0)
 
 
 def solution(mesh):

time: 224 us -> 184 us (0.82)
  blocking collectives: 128 us -> 88.5 us
    psum x1 -> x0, blocking collectives: 128 us -> none  [body(): return lax.psum(running, 'module')]
    all_gather x0 -> x1, blocking collectives: none -> 88.5 us  [body(): return jnp.sum(lax.all_gather(running, 'module'), axis=0)]
where the time goes in v2:
time: 184 us
  blocking collectives  88.5 us (48%)
  waiting for transfers between devices  70.5 us (38%)
  local copies, waits for them, and re-layouts  8.53 us (5%)
  starting transfers between devices  7.6 us (4%)
  other arithmetic  6.86 us (4%)
    all_gather x1, blocking collectives, body(): return jnp.sum(lax.all_gather(running, 'module'), axis=0)  88.5 us
    all_to_all x1, waiting for transfers between devices, body(): lax.all_to_all(outgoing, 'module', split_axis=0, concat_axis=3, tiled=True)  70.5 us
    all_to_all x1, starting transfers between devices, body(): lax.all_to_all(outgoing, 'module', split_axis=0, concat_axis=3, tiled=True)  7.6 us
    another operation x4, local copies, waits for them, and re-layouts  4.93 us
    select_n x1, other arithmetic, body(): jnp.where(populated_slots[:, None, None, None], query_grads[safe_index],...  4.75 us
  transfers between devices with their start and end apart: 1, of which 1 were waited for; matrix products, arithmetic and copies ran while one was open for 3% of the time, Pallas kernels for 0%

profile of v2, /device:TPU:0, one launch (start us, length us, event | category | flops | bytes accessed | tf_op | source)
XLA Modules:
  0.0 183.9 jit_solution(4197467513037245854)
XLA Ops:
  0.0 0.0 copy-start
  0.0 0.8 broadcast_maximum_fusion
  0.8 0.7 broadcast_compare_fusion
  1.5 0.1 broadcast_in_dim.24
  1.6 0.0 copy-done
  1.6 2.8 %gather_fusion = f32[32,32,8,128]{3,2,1,0:T(8,128)} fusion(f32[16,32,8,128]{3,2,1,0:T(8,128)S(1)} %copy-done, s32[1024]{0:T(1024)S(1)} %pad_clamp_fusion), kind=kCustom, calls=%fused_computation | custom fusion | bytes 8388736 | tf_op jit(solution)/shard_map/gather | solution.py:53
  4.4 4.8 %broadcast_select_fusion = f32[16,2,32,8,128]{4,3,2,1,0:T(8,128)} fusion(f32[16,2,32,8,128]{4,3,2,1,0:T(8,128)} %bitcast.81, pred[16,2]{1,0:T(8,128)(4,1)S(1)} %broadcast_in_dim.24), kind=kLoop, calls=%fused_computation.37 | loop fusion | flops 1048576 | bytes 8388640 | tf_op jit(solution)/shard_map/jit(_where)/select_n | solution.py:53
  9.1 0.0 copy-start.4
  9.1 0.0 copy-start.2
  9.1 0.0 copy-start.3
  9.1 7.6 %all-to-all-start = ((f32[16,2,32,8,128]{4,3,2,1,0:T(8,128)}), f32[16,2,32,8,128]{4,3,2,1,0:T(8,128)}, u32[]{:S(2)}, u32[]{:S(2)}) async-start(f32[16,2,32,8,128]{4,3,2,1,0:T(8,128)} %broadcast_select_fusion), calls=%async_computation | async-start | bytes 8388608 | tf_op jit(solution)/shard_map/all_to_all | solution.py:55
  16.7 0.0 copy-done.4
  16.7 0.1 dynamic_slice.11
  16.8 0.6 fusion.24
  18.7 0.0 copy-done.2
  18.8 0.0 copy-done.3
  18.8 2.5 %conditional.6 = (f32[64,128,128]{1,2,0:T(8,128)}) conditional(s32[]{:T(128)} %convert_element_type.9, () %tuple.34, (f32[2,64,128,128]{3,2,1,0:T(8,128)}, f32[128,128]{1,0:T(8,128)S(1)}, f32[128,128]{1,0:T(8,128)S(1)}) %tuple.35), branch_computations={%region_5.6_spmd, %region_6.0_spmd} | conditional | flops 3221225472 | bytes 16908296 | solution.py:42
  18.8 2.4 %broadcast.55 = f32[64,128,128]{1,2,0:T(8,128)} broadcast(f32[]{:T(128)} %constant.18.clone), dimensions={} | broadcast | bytes 4194308 | tf_op jit(solution)/shard_map/broadcast.4
  21.2 0.0 copy-start.1
  21.2 0.0 copy-start.5
  21.3 2.5 %conditional.4 = (f32[64,128,128]{1,2,0:T(8,128)}) conditional(s32[]{:T(128)} %convert_element_type.8, () %tuple.30, (f32[2,64,128,128]{3,2,1,0:T(8,128)}, f32[128,128]{1,0:T(8,128)S(1)}, f32[128,128]{1,0:T(8,128)S(1)}) %tuple.31), branch_computations={%region_0.0_spmd, %region_1.0_spmd} | conditional | flops 3221225472 | bytes 16908296 | solution.py:42
  21.3 2.5 %broadcast.51 = f32[64,128,128]{1,2,0:T(8,128)} broadcast(f32[]{:T(128)} %constant.8.clone), dimensions={} | broadcast | bytes 4194308 | tf_op jit(solution)/shard_map/broadcast.2
  23.7 70.5 %all-to-all-done = f32[16,2,32,8,128]{4,3,2,1,0:T(8,128)} async-done(((f32[16,2,32,8,128]{4,3,2,1,0:T(8,128)}), f32[16,2,32,8,128]{4,3,2,1,0:T(8,128)}, u32[]{:S(2)}, u32[]{:S(2)}) %all-to-all-start) | async-done | bytes 4194336 | tf_op jit(solution)/shard_map/all_to_all | solution.py:55
  94.3 0.0 copy-done.1
  94.3 0.0 copy-done.5
  94.3 0.2 conditional.7
  94.5 0.2 conditional.5
  94.7 88.5 %all-gather = f32[512,64]{1,0:T(8,128)S(1)} all-gather(f32[32,64]{1,0:T(8,128)S(1)} %add.25), channel_id=2, replica_groups=mesh['group'=2,'module'=16] {'module'}, dimensions={0}, use_global_device_ids=true | all-gather | bytes 139264 | tf_op jit(solution)/shard_map/all_gather | solution.py:72
  183.3 0.6 reduce_sum.27
  (5 shorter events, 0.0 us)
Async XLA Ops:
  0.0 1.6 copy-start
  9.1 7.6 %copy-start.4 = (s32[32]{0:T(128)S(1)}, s32[32]{0:T(128)}, u32[]{:S(2)}) copy-start(s32[32]{0:T(128)} %param.21) | copy-start | bytes 388
  9.1 9.6 %copy-start.2 = (f32[2,128,128]{2,1,0:T(8,128)S(1)}, f32[2,128,128]{2,1,0:T(8,128)}, u32[]{:S(2)}) copy-start(f32[2,128,128]{2,1,0:T(8,128)} %param.17) | copy-start | bytes 393220
  9.1 9.6 %copy-start.3 = (f32[2,128,128]{2,1,0:T(8,128)S(1)}, f32[2,128,128]{2,1,0:T(8,128)}, u32[]{:S(2)}) copy-start(f32[2,128,128]{2,1,0:T(8,128)} %param.18) | copy-start | bytes 393220
  9.1 85.1 %all-to-all-start = ((f32[16,2,32,8,128]{4,3,2,1,0:T(8,128)}), f32[16,2,32,8,128]{4,3,2,1,0:T(8,128)}, u32[]{:S(2)}, u32[]{:S(2)}) async-start(f32[16,2,32,8,128]{4,3,2,1,0:T(8,128)} %broadcast_select_fusion), calls=%async_computation | async-start | bytes 8388608 | tf_op jit(solution)/shard_map/all_to_all | solution.py:55
  21.2 73.0 %copy-start.1 = (f32[2,128,128]{2,1,0:T(8,128)S(1)}, f32[2,128,128]{2,1,0:T(8,128)}, u32[]{:S(2)}) copy-start(f32[2,128,128]{2,1,0:T(8,128)} %param.19) | copy-start | bytes 393220
  21.2 73.0 %copy-start.5 = (s32[16]{0:T(128)S(1)}, s32[16]{0:T(128)}, u32[]{:S(2)}) copy-start(s32[16]{0:T(128)} %param.20) | copy-start | bytes 196
